TPU v7x, 32 devices: a whole 2x2x4 slice. The times are simulated.
32 devices in a mesh: seq: 4 (over y, x), ctx: 8 (over z, core).
Axes of the slice: x: 2, y: 2, z: 4, core: 2. Of those that a mesh axis runs over, the one named last changes fastest.
Arguments:
- hidden_in: bfloat16 [16, 1024, 768], P('seq', 'ctx'), may hold values from -6 to 6
- cotangent: bfloat16 [16, 1024, 768], P('seq', 'ctx'), may hold values from -6 to 6
- segments: int32 [16, 1024], P('seq', 'ctx'), may hold values from 0 to 3, never falling along the last dimension, each value on 1 to 512 neighbouring positions
- qkv_weight: bfloat16 [768, 2304], P('seq'), may hold values from -0.21875 to 0.21875
- query_bias: bfloat16 [768], P('seq'), may hold values from -3 to 3
- value_bias: bfloat16 [768], P('seq'), may hold values from -0.29882812 to 0.29882812
- out_weight: bfloat16 [768, 768], P('seq'), may hold values from -1.75 to 1.75
- out_bias: bfloat16 [768], P('seq'), may hold values from -2 to 2
- first_gain: bfloat16 [768], P('seq'), may hold values from 0.5 to 1.5
- first_shift: bfloat16 [768], P('seq'), may hold values from -2 to 2
- inner_weight: bfloat16 [768, 3072], P('seq'), may hold values from -0.21875 to 0.21875
- inner_bias: bfloat16 [3072], P('seq'), may hold values from -3 to 3
- outer_weight: bfloat16 [3072, 768], P('seq'), may hold values from -0.21875 to 0.21875
- outer_bias: bfloat16 [768], P('seq'), may hold values from -2 to 2
- second_gain: bfloat16 [768], P('seq'), may hold values from 0.5 to 1.5
- second_shift: bfloat16 [768], P('seq'), may hold values from -2 to 2
Outputs:
- output: bfloat16 [16, 1024, 768], P('seq', 'ctx')
- grad_input: float32 [16, 1024, 768], P('seq', 'ctx')
- grad_qkv_weight: float32 [768, 2304], P('seq')
- grad_query_bias: float32 [768], P('seq')
- grad_value_bias: float32 [768], P('seq')
- grad_out_weight: float32 [768, 768], P('seq')
- grad_out_bias: float32 [768], P('seq')
- grad_first_gain: float32 [768], P('seq')
- grad_first_shift: float32 [768], P('seq')
- grad_inner_weight: float32 [768, 3072], P('seq')
- grad_inner_bias: float32 [3072], P('seq')
- grad_outer_weight: float32 [3072, 768], P('seq')
- grad_outer_bias: float32 [768], P('seq')
- grad_second_gain: float32 [768], P('seq')
- grad_second_shift: float32 [768], P('seq')
Inputs may be any that keep to these rules, and one draw needn't show every extreme that they name: `segments`: in each sequence the document numbers never fall along the positions; a document holds 1 to 512 positions, and some document holds exactly 512; attention joins only positions of one document of one sequence.
All inputs are finite; a program needn't handle non-finite values.
Results may differ from a plain program's by a relative error of at most 0.035.
Values may be sent and summed in bfloat16 or wider, within the bound.
A program may use at most 320 MiB of HBM per device.

v0:
```python
from functools import partial
import jax
import jax.numpy as jnp
from jax import lax
from jax.sharding import PartitionSpec as P

HEADS = 12
HEAD_DIM = 64
norm_epsilon = 1e-12


def norm_forward(matrix, gain, shift):
    average = jnp.mean(matrix, axis=-1, keepdims=True)
    centred = matrix - average
    factor = lax.rsqrt(jnp.mean(centred * centred, axis=-1, keepdims=True) + norm_epsilon)
    normed = centred * factor
    return (normed * gain + shift, normed, factor)


def norm_backward(upstream, normed, factor, gain):
    scaled = upstream * gain
    return factor * (
        scaled
        - jnp.mean(scaled, axis=-1, keepdims=True)
        - normed * jnp.mean(scaled * normed, axis=-1, keepdims=True)
    )


def split_heads(matrix):
    groups, positions, widths = matrix.shape
    return jnp.moveaxis(matrix.reshape(groups, positions, HEADS, widths // HEADS), 2, 0)


def join_heads(matrix):
    return jnp.moveaxis(matrix, 0, 2).reshape(
        matrix.shape[1], matrix.shape[2], matrix.shape[0] * matrix.shape[3]
    )


def grads_block(query_one, upstream_one, lse_one, delta_one, key_one, value_one, allowed, scaling):
    scores = (
        jnp.einsum("sqd,skd->sqk", query_one, key_one, preferred_element_type=jnp.float32) * scaling
    )
    probability = jnp.exp(jnp.where(allowed, scores - lse_one[..., None], -1e30))
    grad_probs = jnp.einsum(
        "sqd,skd->sqk", upstream_one, value_one, preferred_element_type=jnp.float32
    )
    grad_scores = (probability * (grad_probs - delta_one[..., None])).astype(jnp.bfloat16)
    grad_query = (
        jnp.einsum("sqk,skd->sqd", grad_scores, key_one, preferred_element_type=jnp.float32)
        * scaling
    )
    grad_key = (
        jnp.einsum("sqk,sqd->skd", grad_scores, query_one, preferred_element_type=jnp.float32)
        * scaling
    )
    grad_value = jnp.einsum(
        "sqk,sqd->skd",
        probability.astype(jnp.bfloat16),
        upstream_one,
        preferred_element_type=jnp.float32,
    )
    return (grad_query, grad_key, grad_value)


def on_device(
    hidden_in,
    cotangent,
    segments,
    qkv_weight,
    query_bias,
    value_bias,
    out_weight,
    out_bias,
    first_gain,
    first_shift,
    inner_weight,
    inner_bias,
    outer_weight,
    outer_bias,
    second_gain,
    second_shift,
):
    groups, positions, model_width = hidden_in.shape
    row_count = groups * positions
    scaling = HEAD_DIM ** (-0.5)
    gathered = (
        lax.all_gather(qkv_weight, "seq", axis=0, tiled=True),
        lax.all_gather(query_bias, "seq", axis=0, tiled=True),
        lax.all_gather(value_bias, "seq", axis=0, tiled=True),
        lax.all_gather(out_weight, "seq", axis=0, tiled=True),
        lax.all_gather(out_bias, "seq", axis=0, tiled=True),
        lax.all_gather(first_gain, "seq", axis=0, tiled=True),
        lax.all_gather(first_shift, "seq", axis=0, tiled=True),
        lax.all_gather(inner_weight, "seq", axis=0, tiled=True),
        lax.all_gather(inner_bias, "seq", axis=0, tiled=True),
        lax.all_gather(outer_weight, "seq", axis=0, tiled=True),
        lax.all_gather(outer_bias, "seq", axis=0, tiled=True),
        lax.all_gather(second_gain, "seq", axis=0, tiled=True),
        lax.all_gather(second_shift, "seq", axis=0, tiled=True),
    )
    (
        qkv_full,
        qbias_full,
        vbias_full,
        out_full,
        obias_full,
        fgain_full,
        fshift_full,
        inner_full,
        ibias_full,
        outer_full,
        ubias_full,
        sgain_full,
        sshift_full,
    ) = gathered
    token_rows = hidden_in.reshape(row_count, model_width)
    projected = jnp.dot(token_rows, qkv_full, preferred_element_type=jnp.float32)
    queries_low = (
        (projected[:, :model_width] + qbias_full)
        .astype(jnp.bfloat16)
        .reshape(groups, positions, model_width)
    )
    keys_low = (
        projected[:, model_width : 2 * model_width]
        .astype(jnp.bfloat16)
        .reshape(groups, positions, model_width)
    )
    values_low = (
        (projected[:, 2 * model_width :] + vbias_full)
        .astype(jnp.bfloat16)
        .reshape(groups, positions, model_width)
    )
    seg_low = segments.astype(jnp.bfloat16)
    query_heads = split_heads(queries_low)
    start_state = (
        jnp.full((HEADS, groups, positions), -1e30, jnp.float32),
        jnp.zeros((HEADS, groups, positions), jnp.float32),
        jnp.zeros((HEADS, groups, positions, HEAD_DIM), jnp.float32),
    )
    key_part = lax.all_gather(keys_low, "ctx", axis=1, tiled=True)
    value_part = lax.all_gather(values_low, "ctx", axis=1, tiled=True)
    seg_part = lax.all_gather(seg_low, "ctx", axis=1, tiled=True)
    fold_allowed = seg_low[:, :, None] == seg_part[:, None, :]

    def per_head(head_item):
        query_one, key_one, value_one, old_max, old_total, old_acc = head_item
        scores = (
            jnp.einsum("sqd,skd->sqk", query_one, key_one, preferred_element_type=jnp.float32)
            * scaling
        )
        scores = jnp.where(fold_allowed, scores, -1e30)
        new_max = jnp.maximum(old_max, jnp.max(scores, axis=-1))
        retain = jnp.exp(old_max - new_max)
        weights = jnp.where(fold_allowed, jnp.exp(scores - new_max[..., None]), 0.0)
        run_total = old_total * retain + jnp.sum(weights, axis=-1)
        run_acc = old_acc * retain[..., None] + jnp.einsum(
            "sqk,skd->sqd",
            weights.astype(jnp.bfloat16),
            value_one,
            preferred_element_type=jnp.float32,
        )
        return (new_max, run_total, run_acc)

    run_max, run_total, run_acc = lax.map(
        per_head,
        (
            query_heads,
            split_heads(key_part),
            split_heads(value_part),
            start_state[0],
            start_state[1],
            start_state[2],
        ),
    )
    out_heads = run_acc / run_total[..., None]
    row_lse = run_max + jnp.log(run_total)
    context_low = join_heads(out_heads).reshape(row_count, model_width).astype(jnp.bfloat16)
    attended = jnp.dot(context_low, out_full, preferred_element_type=jnp.float32) + obias_full
    residual = token_rows.astype(jnp.float32) + attended
    first, first_normed, first_factor = norm_forward(residual, fgain_full, fshift_full)
    first_low = first.astype(jnp.bfloat16)
    inner = jnp.dot(first_low, inner_full, preferred_element_type=jnp.float32) + ibias_full
    active = jax.nn.gelu(inner, approximate=False).astype(jnp.bfloat16)
    branch = jnp.dot(active, outer_full, preferred_element_type=jnp.float32) + ubias_full
    result, second_normed, second_factor = norm_forward(first + branch, sgain_full, sshift_full)
    output = result.astype(jnp.bfloat16).reshape(groups, positions, model_width)
    qkv_back, out_back, inner_back, outer_back, fgain_back, sgain_back = (
        lax.all_gather(qkv_weight, "seq", axis=0, tiled=True),
        lax.all_gather(out_weight, "seq", axis=0, tiled=True),
        lax.all_gather(inner_weight, "seq", axis=0, tiled=True),
        lax.all_gather(outer_weight, "seq", axis=0, tiled=True),
        lax.all_gather(first_gain, "seq", axis=0, tiled=True),
        lax.all_gather(second_gain, "seq", axis=0, tiled=True),
    )
    grad_out = cotangent.reshape(row_count, model_width).astype(jnp.float32)
    grad_second_gain = jnp.sum(grad_out * second_normed, axis=0)
    grad_second_shift = jnp.sum(grad_out, axis=0)
    grad_second = norm_backward(grad_out, second_normed, second_factor, sgain_back)
    grad_branch = grad_second.astype(jnp.bfloat16)
    grad_outer_weight = jnp.einsum(
        "rf,rd->fd", active, grad_branch, preferred_element_type=jnp.float32
    )
    grad_outer_bias = jnp.sum(grad_branch.astype(jnp.float32), axis=0)
    grad_active = jnp.einsum(
        "rd,fd->rf", grad_branch, outer_back, preferred_element_type=jnp.float32
    )
    _, gelu_pull = jax.vjp(partial(jax.nn.gelu, approximate=False), inner)
    grad_inner = gelu_pull(grad_active)[0].astype(jnp.bfloat16)
    grad_inner_weight = jnp.einsum(
        "rd,rf->df", first_low, grad_inner, preferred_element_type=jnp.float32
    )
    grad_inner_bias = jnp.sum(grad_inner.astype(jnp.float32), axis=0)
    grad_first = grad_second + jnp.einsum(
        "rf,df->rd", grad_inner, inner_back, preferred_element_type=jnp.float32
    )
    grad_first_gain = jnp.sum(grad_first * first_normed, axis=0)
    grad_first_shift = jnp.sum(grad_first, axis=0)
    grad_residual = norm_backward(grad_first, first_normed, first_factor, fgain_back)
    grad_attended = grad_residual.astype(jnp.bfloat16)
    grad_out_weight = jnp.einsum(
        "rd,re->de", context_low, grad_attended, preferred_element_type=jnp.float32
    )
    grad_out_bias = jnp.sum(grad_attended.astype(jnp.float32), axis=0)
    grad_context = jnp.einsum(
        "re,de->rd", grad_attended, out_back, preferred_element_type=jnp.float32
    )
    grad_context = grad_context.astype(jnp.bfloat16).reshape(groups, positions, model_width)
    grad_heads = split_heads(grad_context)
    row_delta = jnp.sum(grad_heads.astype(jnp.float32) * out_heads, axis=-1)
    far_keys, far_values, far_segs = (
        lax.all_gather(keys_low, "ctx", axis=1, tiled=True),
        lax.all_gather(values_low, "ctx", axis=1, tiled=True),
        lax.all_gather(seg_low, "ctx", axis=1, tiled=True),
    )
    allowed = seg_low[:, :, None] == far_segs[:, None, :]

    def head_keys(head_item):
        query_one, upstream_one, lse_one, delta_one, key_one, value_one = head_item
        return grads_block(
            query_one, upstream_one, lse_one, delta_one, key_one, value_one, allowed, scaling
        )

    dq_heads, dk_heads, dv_heads = lax.map(
        head_keys,
        (
            query_heads,
            grad_heads,
            row_lse,
            row_delta,
            split_heads(far_keys),
            split_heads(far_values),
        ),
    )
    key_grad, value_grad = (
        lax.psum_scatter(
            join_heads(dk_heads).astype(jnp.bfloat16), "ctx", scatter_dimension=1, tiled=True
        ).astype(jnp.float32),
        lax.psum_scatter(
            join_heads(dv_heads).astype(jnp.bfloat16), "ctx", scatter_dimension=1, tiled=True
        ).astype(jnp.float32),
    )
    query_grad = join_heads(dq_heads)
    query_low_grad = query_grad.reshape(row_count, model_width).astype(jnp.bfloat16)
    key_low_grad = key_grad.reshape(row_count, model_width).astype(jnp.bfloat16)
    value_low_grad = value_grad.reshape(row_count, model_width).astype(jnp.bfloat16)
    grad_projected = jnp.concatenate([query_low_grad, key_low_grad, value_low_grad], axis=1)
    grad_qkv_weight = jnp.einsum(
        "rd,rf->df", token_rows, grad_projected, preferred_element_type=jnp.float32
    )
    grad_query_bias = jnp.sum(query_low_grad.astype(jnp.float32), axis=0)
    grad_value_bias = jnp.sum(value_low_grad.astype(jnp.float32), axis=0)
    grad_input = grad_residual + jnp.einsum(
        "rf,df->rd", grad_projected, qkv_back, preferred_element_type=jnp.float32
    )
    owned = (
        lax.psum_scatter(
            grad_qkv_weight.astype(jnp.bfloat16), "seq", scatter_dimension=0, tiled=True
        ).astype(jnp.float32),
        lax.psum_scatter(
            grad_query_bias.astype(jnp.bfloat16), "seq", scatter_dimension=0, tiled=True
        ).astype(jnp.float32),
        lax.psum_scatter(
            grad_value_bias.astype(jnp.bfloat16), "seq", scatter_dimension=0, tiled=True
        ).astype(jnp.float32),
        lax.psum_scatter(
            grad_out_weight.astype(jnp.bfloat16), "seq", scatter_dimension=0, tiled=True
        ).astype(jnp.float32),
        lax.psum_scatter(
            grad_out_bias.astype(jnp.bfloat16), "seq", scatter_dimension=0, tiled=True
        ).astype(jnp.float32),
        lax.psum_scatter(
            grad_first_gain.astype(jnp.bfloat16), "seq", scatter_dimension=0, tiled=True
        ).astype(jnp.float32),
        lax.psum_scatter(
            grad_first_shift.astype(jnp.bfloat16), "seq", scatter_dimension=0, tiled=True
        ).astype(jnp.float32),
        lax.psum_scatter(
            grad_inner_weight.astype(jnp.bfloat16), "seq", scatter_dimension=0, tiled=True
        ).astype(jnp.float32),
        lax.psum_scatter(
            grad_inner_bias.astype(jnp.bfloat16), "seq", scatter_dimension=0, tiled=True
        ).astype(jnp.float32),
        lax.psum_scatter(
            grad_outer_weight.astype(jnp.bfloat16), "seq", scatter_dimension=0, tiled=True
        ).astype(jnp.float32),
        lax.psum_scatter(
            grad_outer_bias.astype(jnp.bfloat16), "seq", scatter_dimension=0, tiled=True
        ).astype(jnp.float32),
        lax.psum_scatter(
            grad_second_gain.astype(jnp.bfloat16), "seq", scatter_dimension=0, tiled=True
        ).astype(jnp.float32),
        lax.psum_scatter(
            grad_second_shift.astype(jnp.bfloat16), "seq", scatter_dimension=0, tiled=True
        ).astype(jnp.float32),
    )
    summed = (
        lax.psum(owned[0].astype(jnp.bfloat16), "ctx").astype(jnp.float32),
        lax.psum(owned[1].astype(jnp.bfloat16), "ctx").astype(jnp.float32),
        lax.psum(owned[2].astype(jnp.bfloat16), "ctx").astype(jnp.float32),
        lax.psum(owned[3].astype(jnp.bfloat16), "ctx").astype(jnp.float32),
        lax.psum(owned[4].astype(jnp.bfloat16), "ctx").astype(jnp.float32),
        lax.psum(owned[5].astype(jnp.bfloat16), "ctx").astype(jnp.float32),
        lax.psum(owned[6].astype(jnp.bfloat16), "ctx").astype(jnp.float32),
        lax.psum(owned[7].astype(jnp.bfloat16), "ctx").astype(jnp.float32),
        lax.psum(owned[8].astype(jnp.bfloat16), "ctx").astype(jnp.float32),
        lax.psum(owned[9].astype(jnp.bfloat16), "ctx").astype(jnp.float32),
        lax.psum(owned[10].astype(jnp.bfloat16), "ctx").astype(jnp.float32),
        lax.psum(owned[11].astype(jnp.bfloat16), "ctx").astype(jnp.float32),
        lax.psum(owned[12].astype(jnp.bfloat16), "ctx").astype(jnp.float32),
    )
    return (
        output,
        grad_input.reshape(groups, positions, model_width),
        summed[0],
        summed[1],
        summed[2],
        summed[3],
        summed[4],
        summed[5],
        summed[6],
        summed[7],
        summed[8],
        summed[9],
        summed[10],
        summed[11],
        summed[12],
    )


def solution(mesh):
    placed = (
        P("seq", "ctx", None),
        P("seq", "ctx", None),
        P("seq", "ctx"),
        P("seq", None),
        P("seq"),
        P("seq"),
        P("seq", None),
        P("seq"),
        P("seq"),
        P("seq"),
        P("seq", None),
        P("seq"),
        P("seq", None),
        P("seq"),
        P("seq"),
        P("seq"),
    )
    return jax.shard_map(
        on_device,
        mesh=mesh,
        in_specs=placed,
        out_specs=(
            P("seq", "ctx", None),
            P("seq", "ctx", None),
            P("seq", None),
            P("seq"),
            P("seq"),
            P("seq", None),
            P("seq"),
            P("seq"),
            P("seq"),
            P("seq", None),
            P("seq"),
            P("seq", None),
            P("seq"),
            P("seq"),
            P("seq"),
        ),
        check_vma=False,
    )
```

profile of v0, /device:TPU:0, one launch (start us, length us, event | category | flops | bytes accessed | tf_op | source)
XLA Modules:
  0.0 961.4 jit_solution(5188691105644556815)
XLA Ops:
  15.8 17.8 %all-reduce.20 = (bf16[768]{0:T(1024)(128)(2,1)S(1)}, bf16[768]{0:T(1024)(128)(2,1)S(1)}, bf16[768]{0:T(1024)(128)(2,1)S(1)}, bf16[768]{0:T(1024)(128)(2,1)S(1)}...) all-reduce(bf16[768]{0:T(1024)(128)(2,1)S(1)} %dynamic-update-slice, ...), channel_id=1, replica_groups=mesh['seq'=4,'ctx'=8] {'seq'}, use_global_device_ids=true, to_apply=%add | all-reduce | flops 5376 | bytes 21504
  33.7 26.3 %all-gather.8.cloned.1.call-done = bf16[768,2304]{1,0:T(8,128)(2,1)} async-done(((bf16[192,2304]{1,0:T(8,128)(2,1)}), bf16[768,2304]{1,0:T(8,128)(2,1)}) %all-gather.8.cloned.1.call-update) | async-done | bytes 3538960 | tf_op jit(solution)/shard_map/all_gather | solution.py:88
  60.0 4.3 fusion.86
  72.2 11.9 %all_gather.60 = bf16[4,1024]{1,0:T(4,128)(2,1)S(1)} all-gather(bf16[4,128]{1,0:T(4,128)(2,1)S(1)} %convert_element_type.236), channel_id=1, replica_groups=mesh['seq'=4,'ctx'=8] {'ctx'}, dimensions={1}, use_global_device_ids=true | all-gather | bytes 9216 | tf_op jit(solution)/shard_map/all_gather | solution.py:143
  84.1 8.2 all-gather
  96.5 36.3 %all-gather.12.cloned.1.call-done = bf16[4,1024,768]{1,2,0:T(8,128)(2,1)} async-done(((bf16[4,128,768]{1,2,0:T(8,128)(2,1)}), bf16[4,1024,768]{1,2,0:T(8,128)(2,1)}) %all-gather.12.cloned.1.call-update) | async-done | bytes 6291472 | tf_op jit(solution)/shard_map/all_gather | solution.py:142
  132.9 6.7 copy.57
  139.6 58.8 %all-gather.10.cloned.1.call-done = bf16[4,1024,768]{1,2,0:T(8,128)(2,1)} async-done(((bf16[4,128,768]{1,2,0:T(8,128)(2,1)}), bf16[4,1024,768]{1,2,0:T(8,128)(2,1)}) %all-gather.10.cloned.1.call-update) | async-done | bytes 6291472 | tf_op jit(solution)/shard_map/all_gather | solution.py:141
  198.4 6.7 copy.56
  205.1 51.8 %while.30 = (s32[]{:T(128)}, f32[12,4,128]{2,1,0:T(4,128)S(1)}, f32[12,4,128]{2,1,0:T(4,128)S(1)}, f32[12,4,128,64]{2,1,3,0:T(4,128)S(1)}, bf16[12,4,128,64]{2,3...) while((s32[]{:T(128)}, f32[12,4,128]{2,1,0:T(4,128)S(1)}, ...), condition=%wide.region_3.4_spmd.clone, body=%wide.region_0.3_spmd.clone.sunk | while | flops 142641664 | bytes 7852653 | solution.py:165
  258.0 2.6 fusion.83
  261.0 23.9 %all-gather.16.cloned.1.call-done = bf16[768,3072]{1,0:T(8,128)(2,1)} async-done(((bf16[192,3072]{1,0:T(8,128)(2,1)}), bf16[768,3072]{1,0:T(8,128)(2,1)}) %all-gather.16.cloned.1.call-update) | async-done | bytes 4718608 | tf_op jit(solution)/shard_map/all_gather | solution.py:95
  284.9 19.8 %multiply_convert_fusion.1 = (bf16[512,3072]{1,0:T(8,128)(2,1)}, f32[512,3072]{1,0:T(8,128)}, f32[512,3072]{1,0:T(8,128)}) fusion(f32[3072]{0:T(1024)S(1)} %bitcast.237, bf16[768,3072]{1,0:T(8,128)(2,1)} %all-gather.16.cloned.1.call-done, f32[512,768]{1,0:T(8,128)S(1)} %get-tuple-element.358, f32[768]{0:T(1024)S(1)} %convert_element_type.244, ...), kind=kOutput, calls=%fused_computation.66 | convolution fusion | flops 2521694208 | bytes 22042624 | tf_op jit(solution)/shard_map/dot_general | solution.py:183
  304.7 39.0 %all-gather.18.cloned.1.call-done = bf16[3072,768]{1,0:T(8,128)(2,1)} async-done(((bf16[768,768]{1,0:T(8,128)(2,1)}), bf16[3072,768]{1,0:T(8,128)(2,1)}) %all-gather.18.cloned.1.call-update) | async-done | bytes 4718608 | tf_op jit(solution)/shard_map/all_gather | solution.py:97
  343.7 6.5 fusion.84
  353.2 9.2 fusion.85
  362.4 5.1 multiply_reduce_fusion
  375.0 103.3 %while.31 = (s32[]{:T(128)}, bf16[12,4,128,64]{2,3,1,0:T(8,128)(2,1)}, bf16[12,4,1024,64]{2,3,0,1:T(8,128)(2,1)}, bf16[12,4,1024,64]{2,3,0,1:T(8,128)(2,1)}, bf1...) while((s32[]{:T(128)}, ...), condition=%wide.region_14.15_spmd.clone, body=%wide.region_13.14_spmd.clone.sunk | while | flops 340033536 | bytes 13657221 | solution.py:244
  381.8 2.2 fusion.138
  390.4 2.2 fusion.138
  398.9 2.2 fusion.138
  424.6 2.2 fusion.138
  433.2 2.2 fusion.138
  441.8 2.2 fusion.138
  458.9 2.2 fusion.138
  467.5 2.2 fusion.138
  478.3 10.8 %copy.70 = bf16[4,1024,768]{2,0,1:T(4,128)(2,1)} copy(bf16[4,1024,768]{1,2,0:T(8,128)(2,1)} %bitcast.219) | data formatting | bytes 12582912
  489.0 6.9 copy.100
  496.0 11.0 %copy.72 = bf16[4,1024,768]{2,0,1:T(4,128)(2,1)} copy(bf16[4,1024,768]{1,2,0:T(8,128)(2,1)} %bitcast.220) | data formatting | bytes 12582912
  507.0 7.0 copy.102
  516.8 49.2 %reduce-scatter.19.cloned.1.call-done = bf16[128,3072]{1,0:T(8,128)(2,1)} async-done(((bf16[1024,3072]{1,0:T(8,128)(2,1)}), bf16[128,3072]{1,0:T(8,128)(2,1)}) %reduce-scatter.19.cloned.1.call-update) | async-done | bytes 786448
  569.3 67.2 %reduce-scatter.21.cloned.1.call-done = bf16[128,3072]{1,0:T(8,128)(2,1)} async-done(((bf16[1024,3072]{1,0:T(8,128)(2,1)}), bf16[128,3072]{1,0:T(8,128)(2,1)}) %reduce-scatter.21.cloned.1.call-update) | async-done | bytes 786448
  639.8 2.2 bitcast_dynamic-update-slice_fusion.2
  644.1 5.4 fusion.54
  649.5 5.8 copy.74
  655.4 3.5 convolution_convert_fusion.3
  659.1 7.9 convolution_convert_fusion.1
  667.2 7.4 convolution_convert_fusion
  674.7 26.5 %reduce-scatter.23.cloned.1.call-done = bf16[192,2304]{1,0:T(8,128)(2,1)} async-done(((bf16[768,2304]{1,0:T(8,128)(2,1)}), bf16[192,2304]{1,0:T(8,128)(2,1)}) %reduce-scatter.23.cloned.1.call-update) | async-done | bytes 884752
  701.1 2.3 copy.75
  703.5 29.0 %reduce-scatter.13.cloned.1.call-done = bf16[192,768]{1,0:T(8,128)(2,1)} async-done(((bf16[768,768]{1,0:T(8,128)(2,1)}), bf16[192,768]{1,0:T(8,128)(2,1)}) %reduce-scatter.13.cloned.1.call-update) | async-done | bytes 294928 | tf_op jit(solution)/shard_map/reduce_scatter | solution.py:286
  732.5 60.1 %reduce-scatter.15.cloned.1.call-done = bf16[192,3072]{1,0:T(8,128)(2,1)} async-done(((bf16[768,3072]{1,0:T(8,128)(2,1)}), bf16[192,3072]{1,0:T(8,128)(2,1)}) %reduce-scatter.15.cloned.1.call-update) | async-done | bytes 1179664 | tf_op jit(solution)/shard_map/reduce_scatter | solution.py:298
  792.6 60.0 %reduce-scatter.17.cloned.1.call-done = bf16[768,768]{1,0:T(8,128)(2,1)} async-done(((bf16[3072,768]{1,0:T(8,128)(2,1)}), bf16[768,768]{1,0:T(8,128)(2,1)}) %reduce-scatter.17.cloned.1.call-update) | async-done | bytes 1179664 | tf_op jit(solution)/shard_map/reduce_scatter | solution.py:304
  856.1 15.5 %all-reduce.19 = (bf16[768]{0:T(1024)(128)(2,1)S(1)}, bf16[768]{0:T(1024)(128)(2,1)S(1)}, bf16[768]{0:T(1024)(128)(2,1)S(1)}, bf16[768]{0:T(1024)(128)(2,1)S(1)}...) all-reduce(bf16[768]{0:T(1024)(128)(2,1)S(1)} %dynamic-update-slice, ...), channel_id=1, replica_groups=mesh['seq'=4,'ctx'=8] {'seq'}, use_global_device_ids=true, to_apply=%add.7 | all-reduce | flops 9984 | bytes 39936
  872.3 15.2 %all-reduce.17 = (bf16[192]{0:T(256)(128)(2,1)S(1)}, bf16[192]{0:T(256)(128)(2,1)S(1)}, bf16[192]{0:T(256)(128)(2,1)S(1)}, bf16[192]{0:T(256)(128)(2,1)S(1)}, bf...) all-reduce(bf16[192]{0:T(256)(128)(2,1)S(1)} %dynamic-slice.9, ...), channel_id=1, replica_groups=mesh['seq'=4,'ctx'=8] {'ctx'}, use_global_device_ids=true, to_apply=%region_21.22 | all-reduce | flops 2304 | bytes 9216 | tf_op jit(solution)/shard_map/psum | solution.py:319
  893.8 5.9 convolution_add_fusion.1
  899.7 47.9 %all-reduce.23.cloned.1.call-done = (bf16[192,2304]{0,1:T(8,128)(2,1)}, bf16[192,768]{1,0:T(8,128)(2,1)}, bf16[192,3072]{1,0:T(8,128)(2,1)}, bf16[768,768]{1,0:T(8,128)(2,1)}) async-done(((bf16[192,2304]{0,1:T(8,128)(2,1)}, bf16[192,768]{1,0:T(8,128)(2,1)}, bf16[192,3072]{1,0:T(8,128)(2,1)}, bf16[768,768]{1,0:T(8,128)(2,1)}), (bf16[192,2304]{0,1:T(8,128)(2,1)}, bf16[192,768]{1,0:T(8,128)(2,1)}, ...) | async-done | bytes 3538960 | tf_op jit(solution)/shard_map/psum | solution.py:318
  947.6 3.0 convert_element_type.284
  (309 shorter events, 193.8 us)
Async XLA Ops:
  7.2 52.8 %all-gather.8.cloned.1.call-start = ((), (), s32[]{:S(2)}) async-start(), calls=%async_computation.6 | async-start | bytes 4423680 | tf_op jit(solution)/shard_map/all_gather | solution.py:88
  7.9 125.0 %all-gather.12.cloned.1.call-start = ((), (), s32[]{:S(2)}) async-start(), calls=%async_computation.8 | async-start | bytes 7077888 | tf_op jit(solution)/shard_map/all_gather | solution.py:142
  64.2 2.1 copy-start.6
  67.5 130.9 %all-gather.10.cloned.1.call-start = ((), (), s32[]{:S(2)}) async-start(), calls=%async_computation.7 | async-start | bytes 7077888 | tf_op jit(solution)/shard_map/all_gather | solution.py:141
  69.1 3.1 copy-start.12
  69.1 15.0 %copy-start.13 = (bf16[768]{0:T(1024)(128)(2,1)S(1)}, bf16[768]{0:T(1024)(128)(2,1)}, u32[]{:S(2)}) copy-start(bf16[768]{0:T(1024)(128)(2,1)} %param.31) | copy-start | bytes 4612
  69.1 23.2 %copy-start = (bf16[4,128,768]{2,1,0:T(8,128)(2,1)S(1)}, bf16[4,128,768]{2,1,0:T(8,128)(2,1)}, u32[]{:S(2)}) copy-start(bf16[4,128,768]{2,1,0:T(8,128)(2,1)} %param.21) | copy-start | bytes 2359300
  70.3 187.0 %all-gather.14.cloned.1.call-start = ((), (), s32[]{:S(2)}) async-start(), calls=%async_computation.9 | async-start | bytes 1474560 | tf_op jit(solution)/shard_map/all_gather | solution.py:91
  70.9 214.0 %all-gather.16.cloned.1.call-start = ((), (), s32[]{:S(2)}) async-start(), calls=%async_computation.10 | async-start | bytes 5898240 | tf_op jit(solution)/shard_map/all_gather | solution.py:95
  71.5 272.2 %all-gather.18.cloned.1.call-start = ((), (), s32[]{:S(2)}) async-start(), calls=%async_computation.11 | async-start | bytes 5898240 | tf_op jit(solution)/shard_map/all_gather | solution.py:97
  72.0 493.9 %reduce-scatter.19.cloned.1.call-start = ((), (), s32[]{:S(2)}) async-start(), calls=%async_computation.15 | async-start | bytes 7077888
  256.9 1.1 copy-start.5
  257.2 3.4 copy-start.7
  260.7 44.0 %copy-start.3 = (f32[512,768]{1,0:T(8,128)}, f32[512,768]{1,0:T(8,128)S(1)}, u32[]{:S(2)}) copy-start(f32[512,768]{1,0:T(8,128)S(1)} %get-tuple-element.358) | copy-start | bytes 4718596
  350.5 2.8 copy-start.14
  351.1 11.3 %slice-start = ((s8[4718592]{0:T(1024)(128)(4,1)}), s8[4194304]{0:T(1024)(128)(4,1)S(1)}, s32[]{:S(2)}) async-start(s8[4718592]{0:T(1024)(128)(4,1)} %bitcast.239), calls=%async_computation.19 | async-start | bytes 8388608
  351.7 10.7 %copy-start.8 = (f32[512,768]{1,0:T(8,128)}, f32[512,768]{1,0:T(8,128)S(1)}, u32[]{:S(2)}) copy-start(f32[512,768]{1,0:T(8,128)S(1)} %get-tuple-element.340) | copy-start | bytes 4718596
  353.2 9.2 copy-start.4
  353.2 9.2 slice-start.1
  367.6 1.7 copy-start.15
  368.1 1.1 copy-start.1
  496.0 140.5 %reduce-scatter.21.cloned.1.call-start = ((), (), s32[]{:S(2)}) async-start(), calls=%async_computation.16 | async-start | bytes 7077888
  514.0 187.1 %reduce-scatter.23.cloned.1.call-start = ((), (), s32[]{:S(2)}) async-start(), calls=%async_computation.17 | async-start | bytes 4423680
  639.8 4.3 copy-start.16
  655.4 77.1 %reduce-scatter.13.cloned.1.call-start = ((), (), s32[]{:S(2)}) async-start(), calls=%async_computation.12 | async-start | bytes 1474560 | tf_op jit(solution)/shard_map/reduce_scatter | solution.py:286
  658.9 133.7 %reduce-scatter.15.cloned.1.call-start = ((), (), s32[]{:S(2)}) async-start(), calls=%async_computation.13 | async-start | bytes 5898240 | tf_op jit(solution)/shard_map/reduce_scatter | solution.py:298
  667.1 185.5 %reduce-scatter.17.cloned.1.call-start = ((), (), s32[]{:S(2)}) async-start(), calls=%async_computation.14 | async-start | bytes 5898240 | tf_op jit(solution)/shard_map/reduce_scatter | solution.py:304
  674.6 273.0 %all-reduce.23.cloned.1.call-start = ((), (), s32[]{:S(2)}) async-start(), calls=%async_computation.18 | async-start | bytes 7667712 | tf_op jit(solution)/shard_map/psum | solution.py:318
  703.4 150.6 %copy-start.17 = (bf16[192]{0:T(256)(128)(2,1)S(1)}, bf16[192]{0:T(256)(128)(2,1)}, u32[]{:S(2)}) copy-start(bf16[192]{0:T(256)(128)(2,1)} %param.35) | copy-start | bytes 1156
  856.1 37.7 %copy-start.2 = (f32[512,768]{1,0:T(8,128)S(1)}, f32[512,768]{1,0:T(8,128)}, u32[]{:S(2)}) copy-start(f32[512,768]{1,0:T(8,128)} %copy-done.1) | copy-start | bytes 4718596
  947.6 3.0 copy-start.9
  950.7 1.7 copy-start.10
  952.3 1.6 copy-start.11
Sparse Core Ops, SparseCore 0:
  9.9 50.0 all-gather.7
  67.7 65.1 all-gather.11
  135.0 63.2 all-gather.9
  200.1 25.9 all-gather.13
  227.7 57.1 all-gather.15
  286.6 57.0 all-gather.17
  496.1 69.7 reduce-scatter.18
  568.2 68.1 reduce-scatter.20
  655.5 45.5 reduce-scatter.22
  703.9 28.5 reduce-scatter.12
  735.5 57.0 reduce-scatter.14
  795.4 57.0 reduce-scatter.16
  855.8 91.8 all-reduce.22
where the time goes:
time: 970 us; the launch traced here: 961 us
  waiting for transfers between devices  527 us (54%)
  matrix products  222 us (23%)
  local copies, waits for them, and re-layouts  98.2 us (10%)
  blocking collectives  68.6 us (7%)
  other arithmetic  27.7 us (3%)
  between operations  16.5 us (2%)
    unnamed x16, waiting for transfers between devices  145 us
    unnamed x81, local copies, waits for them, and re-layouts  80.3 us
    reduce_scatter x1, waiting for transfers between devices, on_device(): lax.psum_scatter(grad_inner_weight.astype(jnp.bfloat16), 'seq', scatter_d...  60.1 us
    reduce_scatter x1, waiting for transfers between devices, on_device(): lax.psum_scatter(grad_outer_weight.astype(jnp.bfloat16), 'seq', scatter_d...  60 us
    all_gather x1, waiting for transfers between devices, on_device(): key_part = lax.all_gather(keys_low, 'ctx', axis=1, tiled=True)  58.8 us
    psum x1, waiting for transfers between devices, on_device(): lax.psum(owned[0].astype(jnp.bfloat16), 'ctx').astype(jnp.float32)  47.9 us
    all_gather x1, waiting for transfers between devices, on_device(): lax.all_gather(outer_weight, 'seq', axis=0, tiled=True)  39 us
    all_gather x1, waiting for transfers between devices, on_device(): value_part = lax.all_gather(values_low, 'ctx', axis=1, tiled=True)  36.3 us
  transfers between devices with their start and end apart: 13, of which 12 were waited for; matrix products, arithmetic and copies ran while one was open for 17% of the time, Pallas kernels for 0%

commit v1 on v0

--- a/solution.py
+++ b/solution.py
@@ -314,8 +314,13 @@
             grad_second_shift.astype(jnp.bfloat16), "seq", scatter_dimension=0, tiled=True
         ).astype(jnp.float32),
     )
+
+    def heads_supply(block_here, axis_tag):
+        piece_next = lax.all_gather(block_here, axis_tag)
+        return jnp.sum(piece_next, axis=0)
+
     summed = (
-        lax.psum(owned[0].astype(jnp.bfloat16), "ctx").astype(jnp.float32),
+        heads_supply(owned[0].astype(jnp.bfloat16), "ctx").astype(jnp.float32),
         lax.psum(owned[1].astype(jnp.bfloat16), "ctx").astype(jnp.float32),
         lax.psum(owned[2].astype(jnp.bfloat16), "ctx").astype(jnp.float32),
         lax.psum(owned[3].astype(jnp.bfloat16), "ctx").astype(jnp.float32),

time: 970 us -> 1000 us (1.031)
  waiting for transfers between devices: 527 us -> 558 us
    reduce_scatter x0 -> x1, waiting for transfers between devices: none -> 50.1 us  [on_device(): lax.psum_scatter(grad_qkv_weight.astype(jnp.bfloat16), 'seq', scatter_dim...]
    unnamed x16, waiting for transfers between devices: 145 us -> 99.4 us
    all_gather x0 -> x1, waiting for transfers between devices: none -> 23.4 us  [heads_supply(): piece_next = lax.all_gather(block_here, axis_tag)]
    psum x1, waiting for transfers between devices: 47.9 us -> 69.6 us  [on_device(): lax.psum(owned[3].astype(jnp.bfloat16), 'ctx').astype(jnp.float32)]
    reduce_scatter x1, waiting for transfers between devices: 29 us -> 11.2 us  [on_device(): lax.psum_scatter(grad_out_weight.astype(jnp.bfloat16), 'seq', scatter_dim...]
    unnamed x81 -> x79, local copies, waits for them, and re-layouts: 80.3 us -> 77.6 us
  transfers between devices with their start and end apart: 13 -> 14, of which waited for: 12 -> 13; matrix products, arithmetic and copies ran while one was open for 17% -> 18% of each run, Pallas kernels for 0% -> 0%
where the time goes in v1:
time: 1000 us; the launch traced here: 995 us
  waiting for transfers between devices  558 us (56%)
  matrix products  221 us (22%)
  local copies, waits for them, and re-layouts  95.6 us (10%)
  blocking collectives  68.7 us (7%)
  other arithmetic  33.4 us (3%)
  between operations  16.5 us (2%)
    unnamed x16, waiting for transfers between devices  99.4 us
    unnamed x79, local copies, waits for them, and re-layouts  77.6 us
    psum x1, waiting for transfers between devices, on_device(): lax.psum(owned[3].astype(jnp.bfloat16), 'ctx').astype(jnp.float32)  69.6 us
    reduce_scatter x1, waiting for transfers between devices, on_device(): lax.psum_scatter(grad_outer_weight.astype(jnp.bfloat16), 'seq', scatter_d...  60.1 us
    reduce_scatter x1, waiting for transfers between devices, on_device(): lax.psum_scatter(grad_inner_weight.astype(jnp.bfloat16), 'seq', scatter_d...  59.9 us
    all_gather x1, waiting for transfers between devices, on_device(): key_part = lax.all_gather(keys_low, 'ctx', axis=1, tiled=True)  58.8 us
    reduce_scatter x1, waiting for transfers between devices, on_device(): lax.psum_scatter(grad_qkv_weight.astype(jnp.bfloat16), 'seq', scatter_dim...  50.1 us
    all_gather x1, waiting for transfers between devices, on_device(): lax.all_gather(outer_weight, 'seq', axis=0, tiled=True)  39 us
  transfers between devices with their start and end apart: 14, of which 13 were waited for; matrix products, arithmetic and copies ran while one was open for 18% of the time, Pallas kernels for 0%

profile of v1, /device:TPU:0, one launch (start us, length us, event | category | flops | bytes accessed | tf_op | source)
XLA Modules:
  0.0 995.4 jit_solution(7667257408375620933)
XLA Ops:
  15.8 17.8 %all-reduce.20 = (bf16[768]{0:T(1024)(128)(2,1)S(1)}, bf16[768]{0:T(1024)(128)(2,1)S(1)}, bf16[768]{0:T(1024)(128)(2,1)S(1)}, bf16[768]{0:T(1024)(128)(2,1)S(1)}...) all-reduce(bf16[768]{0:T(1024)(128)(2,1)S(1)} %dynamic-update-slice, ...), channel_id=1, replica_groups=mesh['seq'=4,'ctx'=8] {'seq'}, use_global_device_ids=true, to_apply=%add.2 | all-reduce | flops 5376 | bytes 21504
  33.7 26.3 %all-gather.10.cloned.1.call-done = bf16[768,2304]{1,0:T(8,128)(2,1)} async-done(((bf16[192,2304]{1,0:T(8,128)(2,1)}), bf16[768,2304]{1,0:T(8,128)(2,1)}) %all-gather.10.cloned.1.call-update) | async-done | bytes 3538960 | tf_op jit(solution)/shard_map/all_gather | solution.py:88
  60.0 4.3 fusion.86
  72.2 11.9 %all_gather.66 = bf16[4,1024]{1,0:T(4,128)(2,1)S(1)} all-gather(bf16[4,128]{1,0:T(4,128)(2,1)S(1)} %convert_element_type.238), channel_id=1, replica_groups=mesh['seq'=4,'ctx'=8] {'ctx'}, dimensions={1}, use_global_device_ids=true | all-gather | bytes 9216 | tf_op jit(solution)/shard_map/all_gather | solution.py:143
  84.1 8.2 all-gather.1
  96.5 36.3 %all-gather.14.cloned.1.call-done = bf16[4,1024,768]{1,2,0:T(8,128)(2,1)} async-done(((bf16[4,128,768]{1,2,0:T(8,128)(2,1)}), bf16[4,1024,768]{1,2,0:T(8,128)(2,1)}) %all-gather.14.cloned.1.call-update) | async-done | bytes 6291472 | tf_op jit(solution)/shard_map/all_gather | solution.py:142
  132.9 6.7 copy.56
  139.6 58.8 %all-gather.12.cloned.1.call-done = bf16[4,1024,768]{1,2,0:T(8,128)(2,1)} async-done(((bf16[4,128,768]{1,2,0:T(8,128)(2,1)}), bf16[4,1024,768]{1,2,0:T(8,128)(2,1)}) %all-gather.12.cloned.1.call-update) | async-done | bytes 6291472 | tf_op jit(solution)/shard_map/all_gather | solution.py:141
  198.4 6.7 copy.55
  205.1 51.8 %while.30 = (s32[]{:T(128)}, f32[12,4,128]{2,1,0:T(4,128)S(1)}, f32[12,4,128]{2,1,0:T(4,128)S(1)}, f32[12,4,128,64]{2,1,3,0:T(4,128)S(1)}, bf16[12,4,128,64]{2,3...) while((s32[]{:T(128)}, f32[12,4,128]{2,1,0:T(4,128)S(1)}, ...), condition=%wide.region_3.4_spmd.clone, body=%wide.region_0.3_spmd.clone.sunk | while | flops 142641664 | bytes 7852653 | solution.py:165
  258.0 2.6 fusion.83
  261.0 23.9 %all-gather.18.cloned.1.call-done = bf16[768,3072]{1,0:T(8,128)(2,1)} async-done(((bf16[192,3072]{1,0:T(8,128)(2,1)}), bf16[768,3072]{1,0:T(8,128)(2,1)}) %all-gather.18.cloned.1.call-update) | async-done | bytes 4718608 | tf_op jit(solution)/shard_map/all_gather | solution.py:95
  284.9 19.8 %multiply_convert_fusion.1 = (bf16[512,3072]{1,0:T(8,128)(2,1)}, f32[512,3072]{1,0:T(8,128)}, f32[512,3072]{1,0:T(8,128)}) fusion(f32[3072]{0:T(1024)S(1)} %bitcast.239, bf16[768,3072]{1,0:T(8,128)(2,1)} %all-gather.18.cloned.1.call-done, f32[512,768]{1,0:T(8,128)S(1)} %get-tuple-element.312, f32[768]{0:T(1024)S(1)} %convert_element_type.246, ...), kind=kOutput, calls=%fused_computation.66 | convolution fusion | flops 2521694208 | bytes 22042624 | tf_op jit(solution)/shard_map/dot_general | solution.py:183
  304.7 39.0 %all-gather.20.cloned.1.call-done = bf16[3072,768]{1,0:T(8,128)(2,1)} async-done(((bf16[768,768]{1,0:T(8,128)(2,1)}), bf16[3072,768]{1,0:T(8,128)(2,1)}) %all-gather.20.cloned.1.call-update) | async-done | bytes 4718608 | tf_op jit(solution)/shard_map/all_gather | solution.py:97
  343.7 6.5 fusion.84
  353.2 9.2 fusion.85
  362.4 5.1 multiply_reduce_fusion
  375.0 103.5 %while.31 = (s32[]{:T(128)}, bf16[12,4,128,64]{2,3,1,0:T(8,128)(2,1)}, bf16[12,4,1024,64]{2,3,0,1:T(8,128)(2,1)}, bf16[12,4,1024,64]{2,3,0,1:T(8,128)(2,1)}, bf1...) while((s32[]{:T(128)}, ...), condition=%wide.region_14.15_spmd.clone, body=%wide.region_13.14_spmd.clone.sunk | while | flops 340033536 | bytes 13657221 | solution.py:244
  399.0 2.2 fusion.138
  416.2 2.2 fusion.138
  433.4 2.2 fusion.138
  442.0 2.2 fusion.138
  459.1 2.2 fusion.138
  467.7 2.2 fusion.138
  476.3 2.2 fusion.138
  478.5 10.8 %copy.69 = bf16[4,1024,768]{2,0,1:T(4,128)(2,1)} copy(bf16[4,1024,768]{1,2,0:T(8,128)(2,1)} %bitcast.221) | data formatting | bytes 12582912
  489.3 6.9 copy.99
  496.3 11.0 %copy.71 = bf16[4,1024,768]{2,0,1:T(4,128)(2,1)} copy(bf16[4,1024,768]{1,2,0:T(8,128)(2,1)} %bitcast.222) | data formatting | bytes 12582912
  507.2 7.0 copy.101
  515.3 3.2 convolution_convert_fusion.3
  518.6 7.4 convolution_convert_fusion.1
  526.1 7.2 convolution_convert_fusion
  536.3 29.8 %reduce-scatter.19.cloned.1.call-done = bf16[128,3072]{1,0:T(8,128)(2,1)} async-done(((bf16[1024,3072]{1,0:T(8,128)(2,1)}), bf16[128,3072]{1,0:T(8,128)(2,1)}) %reduce-scatter.19.cloned.1.call-update) | async-done | bytes 786448
  569.5 67.2 %reduce-scatter.21.cloned.1.call-done = bf16[128,3072]{1,0:T(8,128)(2,1)} async-done(((bf16[1024,3072]{1,0:T(8,128)(2,1)}), bf16[128,3072]{1,0:T(8,128)(2,1)}) %reduce-scatter.21.cloned.1.call-update) | async-done | bytes 786448
  640.0 2.2 bitcast_dynamic-update-slice_fusion.2
  644.4 5.6 fusion.54
  650.0 5.8 copy.73
  655.9 11.2 %reduce-scatter.13.cloned.1.call-done = bf16[192,768]{1,0:T(8,128)(2,1)} async-done(((bf16[768,768]{1,0:T(8,128)(2,1)}), bf16[192,768]{1,0:T(8,128)(2,1)}) %reduce-scatter.13.cloned.1.call-update) | async-done | bytes 294928 | tf_op jit(solution)/shard_map/reduce_scatter | solution.py:286
  667.1 59.9 %reduce-scatter.15.cloned.1.call-done = bf16[192,3072]{1,0:T(8,128)(2,1)} async-done(((bf16[768,3072]{1,0:T(8,128)(2,1)}), bf16[192,3072]{1,0:T(8,128)(2,1)}) %reduce-scatter.15.cloned.1.call-update) | async-done | bytes 1179664 | tf_op jit(solution)/shard_map/reduce_scatter | solution.py:298
  727.1 60.1 %reduce-scatter.17.cloned.1.call-done = bf16[768,768]{1,0:T(8,128)(2,1)} async-done(((bf16[3072,768]{1,0:T(8,128)(2,1)}), bf16[768,768]{1,0:T(8,128)(2,1)}) %reduce-scatter.17.cloned.1.call-update) | async-done | bytes 1179664 | tf_op jit(solution)/shard_map/reduce_scatter | solution.py:304
  787.3 50.1 %reduce-scatter.23.cloned.1.call-done = bf16[192,2304]{1,0:T(8,128)(2,1)} async-done(((bf16[768,2304]{1,0:T(8,128)(2,1)}), bf16[192,2304]{1,0:T(8,128)(2,1)}) %reduce-scatter.23.cloned.1.call-update) | async-done | bytes 884752 | tf_op jit(solution)/shard_map/reduce_scatter | solution.py:277
  840.6 69.6 %all-reduce.23.cloned.1.call-done = (bf16[192,768]{1,0:T(8,128)(2,1)}, bf16[192,3072]{1,0:T(8,128)(2,1)}, bf16[768,768]{1,0:T(8,128)(2,1)}) async-done(((bf16[192,768]{1,0:T(8,128)(2,1)}, bf16[192,3072]{1,0:T(8,128)(2,1)}, bf16[768,768]{1,0:T(8,128)(2,1)}), (bf16[192,768]{1,0:T(8,128)(2,1)}, bf16[192,3072]{1,0:T(8,128)(2,1)}, bf16[768,768]{1,0:T(8,128)(2,1)})) %all-reduce.23.cloned.1.call-update) | async-done | bytes 2654224 | tf_op jit(solution)/shard_map/psum | solution.py:326
  910.2 3.0 convert_element_type.286
  916.0 16.2 %all-reduce.19 = (bf16[768]{0:T(1024)(128)(2,1)S(1)}, bf16[768]{0:T(1024)(128)(2,1)S(1)}, bf16[768]{0:T(1024)(128)(2,1)S(1)}, bf16[768]{0:T(1024)(128)(2,1)S(1)}...) all-reduce(bf16[768]{0:T(1024)(128)(2,1)S(1)} %dynamic-update-slice, ...), channel_id=1, replica_groups=mesh['seq'=4,'ctx'=8] {'seq'}, use_global_device_ids=true, to_apply=%add.7 | all-reduce | flops 9984 | bytes 39936
  932.9 14.6 %all-reduce.17 = (bf16[192]{0:T(256)(128)(2,1)S(1)}, bf16[192]{0:T(256)(128)(2,1)S(1)}, bf16[192]{0:T(256)(128)(2,1)S(1)}, bf16[192]{0:T(256)(128)(2,1)S(1)}, bf...) all-reduce(bf16[192]{0:T(256)(128)(2,1)S(1)} %dynamic-slice.9, ...), channel_id=1, replica_groups=mesh['seq'=4,'ctx'=8] {'ctx'}, use_global_device_ids=true, to_apply=%region_21.22 | all-reduce | flops 2304 | bytes 9216 | tf_op jit(solution)/shard_map/psum | solution.py:324
  953.8 5.7 convolution_add_fusion.1
  959.5 23.4 %all-gather.22.cloned.1.call-done = bf16[1536,2304]{1,0:T(8,128)(2,1)} async-done(((bf16[192,2304]{1,0:T(8,128)(2,1)}), bf16[1536,2304]{1,0:T(8,128)(2,1)}) %all-gather.22.cloned.1.call-update) | async-done | bytes 7077904 | tf_op jit(solution)/shard_map/all_gather | solution.py:319
  982.9 4.4 reduce_sum.214
  (312 shorter events, 197.0 us)
Async XLA Ops:
  7.2 52.8 %all-gather.10.cloned.1.call-start = ((), (), s32[]{:S(2)}) async-start(), calls=%async_computation.6 | async-start | bytes 4423680 | tf_op jit(solution)/shard_map/all_gather | solution.py:88
  7.9 125.0 %all-gather.14.cloned.1.call-start = ((), (), s32[]{:S(2)}) async-start(), calls=%async_computation.8 | async-start | bytes 7077888 | tf_op jit(solution)/shard_map/all_gather | solution.py:142
  64.2 2.1 copy-start.5
  67.5 130.9 %all-gather.12.cloned.1.call-start = ((), (), s32[]{:S(2)}) async-start(), calls=%async_computation.7 | async-start | bytes 7077888 | tf_op jit(solution)/shard_map/all_gather | solution.py:141
  69.1 3.1 copy-start.12
  69.1 15.0 %copy-start.13 = (bf16[768]{0:T(1024)(128)(2,1)S(1)}, bf16[768]{0:T(1024)(128)(2,1)}, u32[]{:S(2)}) copy-start(bf16[768]{0:T(1024)(128)(2,1)} %param.31) | copy-start | bytes 4612
  69.1 23.2 %copy-start = (bf16[4,128,768]{2,1,0:T(8,128)(2,1)S(1)}, bf16[4,128,768]{2,1,0:T(8,128)(2,1)}, u32[]{:S(2)}) copy-start(bf16[4,128,768]{2,1,0:T(8,128)(2,1)} %param.21) | copy-start | bytes 2359300
  70.3 187.0 %all-gather.16.cloned.1.call-start = ((), (), s32[]{:S(2)}) async-start(), calls=%async_computation.9 | async-start | bytes 1474560 | tf_op jit(solution)/shard_map/all_gather | solution.py:91
  70.9 214.0 %all-gather.18.cloned.1.call-start = ((), (), s32[]{:S(2)}) async-start(), calls=%async_computation.10 | async-start | bytes 5898240 | tf_op jit(solution)/shard_map/all_gather | solution.py:95
  71.5 272.2 %all-gather.20.cloned.1.call-start = ((), (), s32[]{:S(2)}) async-start(), calls=%async_computation.11 | async-start | bytes 5898240 | tf_op jit(solution)/shard_map/all_gather | solution.py:97
  72.0 494.1 %reduce-scatter.19.cloned.1.call-start = ((), (), s32[]{:S(2)}) async-start(), calls=%async_computation.16 | async-start | bytes 7077888
  256.9 1.1 copy-start.4
  257.2 3.4 copy-start.6
  260.7 44.0 %copy-start.2 = (f32[512,768]{1,0:T(8,128)}, f32[512,768]{1,0:T(8,128)S(1)}, u32[]{:S(2)}) copy-start(f32[512,768]{1,0:T(8,128)S(1)} %get-tuple-element.312) | copy-start | bytes 4718596
  350.5 2.8 copy-start.14
  351.1 11.3 %slice-start = ((s8[4718592]{0:T(1024)(128)(4,1)}), s8[4194304]{0:T(1024)(128)(4,1)S(1)}, s32[]{:S(2)}) async-start(s8[4718592]{0:T(1024)(128)(4,1)} %bitcast.241), calls=%async_computation.20 | async-start | bytes 8388608
  351.7 10.7 %copy-start.8 = (f32[512,768]{1,0:T(8,128)}, f32[512,768]{1,0:T(8,128)S(1)}, u32[]{:S(2)}) copy-start(f32[512,768]{1,0:T(8,128)S(1)} %get-tuple-element.294) | copy-start | bytes 4718596
  353.2 9.2 copy-start.3
  353.2 9.2 slice-start.1
  367.6 1.7 copy-start.15
  368.1 1.2 copy-start.1
  496.2 140.5 %reduce-scatter.21.cloned.1.call-start = ((), (), s32[]{:S(2)}) async-start(), calls=%async_computation.17 | async-start | bytes 7077888
  514.2 1.1 copy-start.7
  514.2 152.9 %reduce-scatter.13.cloned.1.call-start = ((), (), s32[]{:S(2)}) async-start(), calls=%async_computation.12 | async-start | bytes 1474560 | tf_op jit(solution)/shard_map/reduce_scatter | solution.py:286
  518.6 208.5 %reduce-scatter.15.cloned.1.call-start = ((), (), s32[]{:S(2)}) async-start(), calls=%async_computation.13 | async-start | bytes 5898240 | tf_op jit(solution)/shard_map/reduce_scatter | solution.py:298
  526.1 261.1 %reduce-scatter.17.cloned.1.call-start = ((), (), s32[]{:S(2)}) async-start(), calls=%async_computation.14 | async-start | bytes 5898240 | tf_op jit(solution)/shard_map/reduce_scatter | solution.py:304
  533.3 304.1 %reduce-scatter.23.cloned.1.call-start = ((), (), s32[]{:S(2)}) async-start(), calls=%async_computation.18 | async-start | bytes 4423680 | tf_op jit(solution)/shard_map/reduce_scatter | solution.py:277
  640.0 4.4 copy-start.16
  655.9 183.1 %copy-start.17 = (bf16[192]{0:T(256)(128)(2,1)S(1)}, bf16[192]{0:T(256)(128)(2,1)}, u32[]{:S(2)}) copy-start(bf16[192]{0:T(256)(128)(2,1)} %param.35) | copy-start | bytes 1156
  655.9 254.3 %all-reduce.23.cloned.1.call-start = ((), (), s32[]{:S(2)}) async-start(), calls=%async_computation.19 | async-start | bytes 5308416 | tf_op jit(solution)/shard_map/psum | solution.py:326
  787.2 195.7 %all-gather.22.cloned.1.call-start = ((), (), s32[]{:S(2)}) async-start(), calls=%async_computation.15 | async-start | bytes 7962624 | tf_op jit(solution)/shard_map/all_gather | solution.py:319
  910.2 3.0 copy-start.9
  913.2 1.6 copy-start.10
  947.5 6.3 copy-start.11
Sparse Core Ops, SparseCore 0:
  9.9 50.0 all-gather.9
  67.7 65.1 all-gather.13
  135.0 63.2 all-gather.11
  200.1 25.9 all-gather.15
  227.7 57.1 all-gather.17
  286.6 57.0 all-gather.19
  496.3 69.7 reduce-scatter.18
  568.5 68.1 reduce-scatter.20
  640.2 26.9 reduce-scatter.12
  670.0 57.0 reduce-scatter.14
  730.1 57.0 reduce-scatter.16
  790.1 47.2 reduce-scatter.22
  840.0 70.1 all-reduce.22
  911.7 71.1 all-gather.21
